TPU v7x, 32 devices: a whole 2x2x4 slice. The times are simulated.
32 devices in a mesh: sec: 8 (over y, x, core), col: 4 (over z).
Axes of the slice: x: 2, y: 2, z: 4, core: 2. Of those that a mesh axis runs over, the one named last changes fastest.
Arguments:
- air_state: float32 [4, 64, 32768], P(None, None, ('sec', 'col')), may hold values from -6 to 6
- air_mix: float32 [64, 32768], P(None, ('sec', 'col')), may hold values from 0.1 to 4
- surface_forcing: float32 [4, 32768], P(None, ('sec', 'col')), may hold values from 0 to 2
- air_mask: int32 [32768], P(('sec', 'col')), may hold values 0 or 1
- ocean_sources: int32 [4, 32768], P(None, ('sec', 'col')), may hold values from 0 to 6143, as said below
- ocean_weights: float32 [4, 32768], P(None, ('sec', 'col')), may hold values from 0.1 to 0.5
- sea_state: float32 [2, 80, 16384], P(None, None, ('sec', 'col')), may hold values from -6 to 6
- sea_mix: float32 [80, 16384], P(None, ('sec', 'col')), may hold values from 0.1 to 4
- ice_cover: float32 [16384], P(('sec', 'col')), may hold values from 0.05 to 0.95
- sea_mask: int32 [16384], P(('sec', 'col')), may hold values 0 or 1
- air_sources: int32 [4, 16384], P(None, ('sec', 'col')), may hold values from 0 to 12287, as said below
- air_weights: float32 [4, 16384], P(None, ('sec', 'col')), may hold values from 0.1 to 0.5
Outputs:
- air_out: float32 [4, 64, 32768], P(None, None, ('sec', 'col'))
- sea_out: float32 [2, 80, 16384], P(None, None, ('sec', 'col'))
- ice_out: float32 [16384], P(('sec', 'col'))
Inputs may be any that keep to these rules, and one draw needn't show every extreme that they name: Section t holds ocean cells t * 2048 to (t + 1) * 2048 - 1 and atmosphere columns t * 4096 to (t + 1) * 4096 - 1. An entry s of ocean_sources names cell s mod 2048 of the section s // 2048 - 1 places after the column's own. An entry s of air_sources names column s mod 4096 of the section s // 4096 - 1 places after the cell's own.
All inputs are finite; a program needn't handle non-finite values. No bound on the sum of `air_mask` or of `sea_mask` on one device may be relied on, other than what follows from the above.
Results may differ from a plain program's by a relative error of at most 0.0001.
Values sent between devices are 32-bit elements; how exact they have to be, the bound alone decides.
No kernel may reach another device: no remote copies, remote signals or barrier semaphores. Data moves between devices by JAX's collectives and lax.ppermute only.
A program may use at most 64 MiB of HBM per device.

v0:
```python
import jax
import jax.numpy as jnp
from jax import lax
from jax.sharding import PartitionSpec as P

STEPS = 2


def extended(value, sides, width):
    for axis, dim in sides:
        peers, length = (lax.axis_size(axis), value.shape[dim])
        up = [(i, (i + 1) % peers) for i in range(peers)]
        down = [(j, i) for i, j in up]
        last = lax.slice_in_dim(value, length - width, length, axis=dim)
        leading = lax.slice_in_dim(value, 0, width, axis=dim)
        before = lax.ppermute(last, axis, up)
        after = lax.ppermute(leading, axis, down)
        value = jnp.concatenate([before, value, after], axis=dim)
    return value


def solve_columns(mixing, right_side):
    column_depth = mixing.shape[0]
    zeros_row = jnp.zeros_like(mixing[0])
    carry_c = zeros_row
    carry_d = jnp.zeros_like(right_side[:, 0])
    ratios = []
    reduced = []
    for depth_index in range(column_depth):
        lower_k = mixing[depth_index - 1] if depth_index > 0 else zeros_row
        upper_k = mixing[depth_index]
        pivot_value = 1.0 + lower_k + upper_k + lower_k * carry_c
        carry_c = -upper_k / pivot_value
        carry_d = (right_side[:, depth_index] + lower_k * carry_d) / pivot_value
        ratios.append(carry_c)
        reduced.append(carry_d)
    current = reduced[-1]
    solved = [current]
    for depth_index in range(column_depth - 2, -1, -1):
        current = reduced[depth_index] - ratios[depth_index] * current
        solved.append(current)
    return jnp.stack(solved[::-1], axis=1)


def remap(values, places, weights):
    return jnp.sum(weights[None] * values[:, places], axis=1)


def surface_fluxes(air_state, air_sea, surface_forcing, air_mask):
    bottom = air_state[:, 0]
    over_sea = air_mask == 1
    skin = jnp.where(over_sea, air_sea[0], surface_forcing[3])
    frozen = jnp.where(over_sea, air_sea[1], 0.0)
    speed = jnp.sqrt(bottom[2] * bottom[2] + bottom[3] * bottom[3] + 1.0)
    coefficient = 0.3 * speed / (1.0 + frozen)
    snow_part = 1.0 / (1.0 + jnp.exp(2.0 * skin))
    return jnp.stack(
        [
            coefficient * (skin - bottom[0]),
            coefficient * (0.5 * jnp.exp(0.3 * skin) - bottom[1]),
            coefficient * bottom[2],
            coefficient * bottom[3],
            surface_forcing[0] / (1.0 + frozen),
            surface_forcing[1] - 0.2 * skin,
            surface_forcing[2] * (1.0 - snow_part),
            surface_forcing[2] * snow_part,
        ]
    )


def air_step(air_state, air_mix, fluxes):
    bottom_add = jnp.stack([fluxes[0], fluxes[1], -fluxes[2], -fluxes[3]])
    return solve_columns(air_mix, air_state.at[:, 0].add(bottom_add))


def sea_step(sea_state, sea_mix, ice_cover, sea_mask, sea_flux):
    stress = jnp.sqrt(sea_flux[2] * sea_flux[2] + sea_flux[3] * sea_flux[3] + 0.01)
    heat = sea_flux[4] + sea_flux[5] - sea_flux[0] - sea_flux[1]
    open_water = 1.0 - ice_cover
    depth_decay = jnp.exp(-jnp.arange(sea_mix.shape[0], dtype=jnp.float32) / 8.0)
    mixing = sea_mix * (1.0 + 2.0 * stress[None, :] * depth_decay[:, None])
    top_add = jnp.stack(
        [0.5 * open_water * heat, 0.3 * open_water * (0.4 * sea_flux[1] - sea_flux[6])]
    )
    solved = solve_columns(mixing, sea_state.at[:, 0].add(top_add))
    wet_cells = sea_mask == 1
    new_state = jnp.where(wet_cells[None, None], solved, sea_state)
    grown = ice_cover / (ice_cover + open_water * jnp.exp(0.5 * heat - 0.8 * sea_flux[7]))
    return (new_state, jnp.where(wet_cells, grown, ice_cover))


def per_device(
    air_state,
    air_mix,
    surface_forcing,
    air_mask,
    ocean_sources,
    ocean_weights,
    sea_state,
    sea_mix,
    ice_cover,
    sea_mask,
    air_sources,
    air_weights,
):
    group_count = lax.axis_size("col")
    air_cols = air_state.shape[2]
    sea_cols = sea_state.shape[2]
    air_span = air_cols * group_count
    for step_index in range(STEPS):
        sea_top = jnp.stack([sea_state[0, 0], ice_cover])
        sea_block = lax.all_gather(sea_top, "col", axis=1, tiled=True)
        sea_nearby = extended(sea_block, (("sec", 1),), sea_cols * group_count)
        air_sea = remap(sea_nearby, ocean_sources, ocean_weights)
        fluxes = surface_fluxes(air_state, air_sea, surface_forcing, air_mask)
        flux_block = lax.all_gather(fluxes, "col", axis=1, tiled=True)
        flux_nearby = extended(flux_block, (("sec", 1),), air_span)
        air_state = air_step(air_state, air_mix, fluxes)
        sea_flux = remap(flux_nearby, air_sources, air_weights)
        sea_state, ice_cover = sea_step(sea_state, sea_mix, ice_cover, sea_mask, sea_flux)
    return (air_state, sea_state, ice_cover)


def solution(mesh):
    placed = (
        P(None, None, ("sec", "col")),
        P(None, ("sec", "col")),
        P(None, ("sec", "col")),
        P(("sec", "col")),
        P(None, ("sec", "col")),
        P(None, ("sec", "col")),
        P(None, None, ("sec", "col")),
        P(None, ("sec", "col")),
        P(("sec", "col")),
        P(("sec", "col")),
        P(None, ("sec", "col")),
        P(None, ("sec", "col")),
    )
    return jax.shard_map(
        per_device,
        mesh=mesh,
        in_specs=placed,
        out_specs=(P(None, None, ("sec", "col")), P(None, None, ("sec", "col")), P(("sec", "col"))),
        check_vma=False,
    )
```

profile of v0, /device:TPU:0, one launch (start us, length us, event | category | flops | bytes accessed | tf_op | source)
XLA Modules:
  0.0 243.3 jit_solution(5167946704040412479)
XLA Ops:
  2.1 14.9 %all_gather.12 = f32[2,2048]{1,0:T(2,128)S(1)} all-gather(f32[2,512]{1,0:T(2,128)S(1)} %pad_maximum_fusion.4), channel_id=1, replica_groups=mesh['sec'=8,'col'=4] {'col'}, dimensions={1}, use_global_device_ids=true | all-gather | bytes 20480 | tf_op jit(solution)/shard_map/all_gather | solution.py:112
  17.5 1.9 fusion.457
  19.5 1.9 fusion.458
  21.5 1.8 fusion.459
  23.3 2.9 %negate_divide_fusion.20 = (f32[1,1024]{1,0:T(1,128)}, f32[1,1024]{1,0:T(1,128)}, f32[1,1024]{1,0:T(1,128)}, f32[1,1024]{1,0:T(1,128)}, f32[1,1024]{1,0:T(1,128)...) fusion(f32[64,1024]{1,0:T(8,128)} %param.21), kind=kLoop, calls=%fused_computation.1316 | loop fusion | flops 260096 | bytes 524288 | tf_op jit(solution)/shard_map/div | solution.py:33
  26.2 3.2 %fusion.452 = (f32[4,1,1024]{2,1,0:T(1,128)S(1)}, f32[4,1,1024]{2,1,0:T(1,128)}, f32[4,1,1024]{2,1,0:T(1,128)}, f32[4,1,1024]{2,1,0:T(1,128)}, f32[4,1,1024]{2,1...) fusion(f32[4,64,1024]{2,1,0:T(8,128)} %param.20), kind=kLoop, calls=%fused_computation.1762 | loop fusion | bytes 622592 | tf_op jit(solution)/shard_map/slice | solution.py:34
  29.4 3.4 %fusion.453 = (f32[4,1,1024]{2,1,0:T(1,128)}, f32[4,1,1024]{2,1,0:T(1,128)}, f32[4,1,1024]{2,1,0:T(1,128)}, f32[4,1,1024]{2,1,0:T(1,128)}, f32[4,1,1024]{2,1,0:T...) fusion(f32[4,64,1024]{2,1,0:T(8,128)} %param.20), kind=kLoop, calls=%fused_computation.1763 | loop fusion | bytes 622592 | tf_op jit(solution)/shard_map/slice | solution.py:34
  32.9 1.9 fusion.456
  35.0 1.4 fusion.455
  36.4 2.3 fusion.454
  38.7 3.3 %fusion.451 = (f32[4,1,1024]{2,1,0:T(1,128)}, f32[4,1,1024]{2,1,0:T(1,128)S(1)}, f32[4,1,1024]{2,1,0:T(1,128)}, f32[4,1,1024]{2,1,0:T(1,128)}, f32[4,1,1024]{2,1...) fusion(f32[4,64,1024]{2,1,0:T(8,128)} %param.20), kind=kLoop, calls=%fused_computation.1761 | loop fusion | bytes 622592 | tf_op jit(solution)/shard_map/slice | solution.py:34
  43.8 1.7 multiply_add_fusion.20
  45.6 1.3 multiply_add_fusion.19
  46.8 1.3 multiply_add_fusion.18
  48.1 1.3 multiply_add_fusion.17
  49.4 1.3 multiply_add_fusion.16
  50.7 1.3 multiply_add_fusion.15
  52.0 1.3 multiply_add_fusion.14
  54.5 1.3 multiply_add_fusion.12
  55.8 1.3 multiply_add_fusion.11
  57.1 1.3 multiply_add_fusion.10
  58.4 1.3 multiply_add_fusion.9
  59.7 1.3 multiply_add_fusion.8
  61.0 1.3 multiply_add_fusion.7
  62.2 1.3 multiply_add_fusion.6
  68.6 1.3 multiply_add_fusion.1
  72.4 1.8 copy.754
  74.1 15.4 %gather_fusion = f32[4096,2]{1,0:T(8,128)} fusion(f32[2,6144]{0,1:T(8,128)S(1)} %copy.754, s32[4096]{0:T(1024)} %bitcast_clamp_fusion), kind=kCustom, calls=%fused_computation | custom fusion | bytes 81920 | tf_op jit(solution)/shard_map/gather | solution.py:46
  89.9 2.0 multiply_reduce_fusion.1
  94.7 13.5 %all_gather.13 = f32[8,4096]{1,0:T(8,128)S(1)} all-gather(f32[8,1024]{1,0:T(8,128)S(1)} %stack.715), channel_id=1, replica_groups=mesh['sec'=8,'col'=4] {'col'}, dimensions={1}, use_global_device_ids=true | all-gather | bytes 163840 | tf_op jit(solution)/shard_map/all_gather | solution.py:116
  109.1 1.9 fusion.91
  111.4 3.7 %multiply_subtract_fusion.103 = (f32[4,1024]{1,0:T(4,128)S(1)}, f32[4,1024]{1,0:T(4,128)}, f32[4,1024]{1,0:T(4,128)}, f32[4,1024]{1,0:T(4,128)}, f32[4,1024]{1,0...) fusion(f32[4,1024]{1,0:T(4,128)S(1)} %get-tuple-element.742, ...), kind=kLoop, calls=%fused_computation.712 | loop fusion | flops 1200128 | bytes 2097152 | tf_op jit(solution)/shard_map/sub | solution.py:40
  115.5 2.2 add_divide_fusion.63
  117.8 3.9 %copy.819 = f32[8,12288]{0,1:T(8,128)} copy(f32[8,12288]{1,0:T(8,128)S(1)} %pad_maximum_fusion) | data formatting | bytes 786432 | tf_op jit(solution)/shard_map/concatenate | solution.py:18
  121.7 8.3 %gather_fusion.1 = f32[2048,8]{1,0:T(8,128)S(1)} fusion(f32[8,12288]{0,1:T(8,128)} %copy.819, s32[2048]{0:T(1024)S(1)} %copy-done.205), kind=kCustom, calls=%fused_computation.1 | custom fusion | bytes 139264 | tf_op jit(solution)/shard_map/gather | solution.py:46
  135.8 13.2 %all_gather.14 = f32[2,2048]{1,0:T(2,128)S(1)} all-gather(f32[2,512]{1,0:T(2,128)S(1)} %pad_maximum_fusion.5), channel_id=1, replica_groups=mesh['sec'=8,'col'=4] {'col'}, dimensions={1}, use_global_device_ids=true | all-gather | bytes 20480 | tf_op jit(solution)/shard_map/all_gather | solution.py:112
  150.5 2.7 %collective-permute-done.4 = f32[2,2048]{1,0:T(2,128)S(1)} collective-permute-done((f32[2,2048]{1,0:T(2,128)S(1)}, f32[2,2048]{1,0:T(2,128)S(1)}, u32[]{:S(2)}, u32[]{:S(2)}) %collective-permute-start.4) | collective-permute-done | bytes 16416 | tf_op jit(solution)/shard_map/ppermute | solution.py:16
  153.9 1.8 copy.901
  155.6 15.4 %gather_fusion.2 = f32[4096,2]{1,0:T(8,128)} fusion(f32[2,6144]{0,1:T(8,128)S(1)} %copy.901, s32[4096]{0:T(1024)} %bitcast_clamp_fusion), kind=kCustom, calls=%fused_computation.2 | custom fusion | bytes 81920 | tf_op jit(solution)/shard_map/gather | solution.py:46
  171.4 2.0 multiply_reduce_fusion
  176.2 13.5 %all_gather.15 = f32[8,4096]{1,0:T(8,128)S(1)} all-gather(f32[8,1024]{1,0:T(8,128)S(1)} %stack.831), channel_id=1, replica_groups=mesh['sec'=8,'col'=4] {'col'}, dimensions={1}, use_global_device_ids=true | all-gather | bytes 163840 | tf_op jit(solution)/shard_map/all_gather | solution.py:116
  190.5 3.1 %add_divide_fusion.38 = (f32[4,1,1024]{2,0,1:T(4,128)S(1)}, f32[4,1,1024]{2,0,1:T(4,128)S(1)}, f32[4,1,1024]{2,0,1:T(4,128)S(1)}, f32[4,1,1024]{2,0,1:T(4,128)S(...) fusion(f32[1024]{0:T(1024)} %bitcast.3545, ...), kind=kLoop, calls=%fused_computation.586 | loop fusion | flops 1093632 | bytes 2232320 | tf_op jit(solution)/shard_map/div | solution.py:34
  193.9 2.0 add_divide_fusion.60
  196.0 2.6 %constant_dynamic-update-slice_fusion.143 = (f32[4,64,1024]{2,0,1:T(4,128)S(1)}, f32[4,1024]{1,0:T(4,128)S(1)}, f32[4,1024]{1,0:T(4,128)S(1)}, f32[4,1024]{1,0:T...) fusion(f32[4,1024]{1,0:T(4,128)S(1)} %get-tuple-element.437, ...), kind=kLoop, calls=%fused_computation.155 | loop fusion | flops 1392639 | bytes 2138112
  199.0 3.4 %constant_dynamic-update-slice_fusion.142 = (f32[4,64,1024]{2,0,1:T(4,128)S(1)}, f32[4,1,1024]{2,0,1:T(4,128)S(1)}, f32[4,1,1024]{2,0,1:T(4,128)S(1)}, f32[4,1,1...) fusion(f32[4,64,1024]{2,0,1:T(4,128)S(1)} %get-tuple-element.40, ...), kind=kLoop, calls=%fused_computation.154 | loop fusion | flops 1454080 | bytes 2519040
  222.3 1.6 copy.904
  223.9 4.2 %copy.902 = f32[8,12288]{0,1:T(8,128)} copy(f32[8,12288]{1,0:T(8,128)S(1)} %pad_maximum_fusion.1) | data formatting | bytes 786432 | tf_op jit(solution)/shard_map/concatenate | solution.py:18
  228.1 8.3 %gather_fusion.3 = f32[2048,8]{1,0:T(8,128)S(1)} fusion(f32[8,12288]{0,1:T(8,128)} %copy.902, s32[2048]{0:T(1024)S(1)} %copy-done.206), kind=kCustom, calls=%fused_computation.3 | custom fusion | bytes 139264 | tf_op jit(solution)/shard_map/gather | solution.py:46
  (814 shorter events, 52.9 us)
Async XLA Ops:
  0.6 41.3 %copy-start.211 = (f32[4,1024]{1,0:T(4,128)S(1)}, f32[4,1024]{1,0:T(4,128)}, u32[]{:S(2)}) copy-start(f32[4,1024]{1,0:T(4,128)} %param.22) | copy-start | bytes 49156
  0.6 41.9 %copy-start.212 = (s32[4,1024]{1,0:T(4,128)S(1)}, s32[4,1024]{1,0:T(4,128)}, u32[]{:S(2)}) copy-start(s32[4,1024]{1,0:T(4,128)} %param.24) | copy-start | bytes 49156
  0.7 42.6 %copy-start.216 = (s32[4,512]{1,0:T(4,128)S(1)}, s32[4,512]{1,0:T(4,128)}, u32[]{:S(2)}) copy-start(s32[4,512]{1,0:T(4,128)} %param.30) | copy-start | bytes 24580
  17.0 54.5 %collective-permute-start.1 = (f32[2,2048]{1,0:T(2,128)S(1)}, f32[2,2048]{1,0:T(2,128)S(1)}, u32[]{:S(2)}, u32[]{:S(2)}) collective-permute-start(f32[2,2048]{1,0:T(2,128)S(1)} %all_gather.12), channel_id=1, source_target_pairs={{4,0},{8,4},{12,8},{16,12},{20,16},{24,20},{28,24},{0,28},{5,1},{9... | collective-permute-start | bytes 49160 | tf_op jit(solution)/shard_map/ppermute | solution.py:17
  17.0 54.6 %collective-permute-start = (f32[2,2048]{1,0:T(2,128)S(1)}, f32[2,2048]{1,0:T(2,128)S(1)}, u32[]{:S(2)}, u32[]{:S(2)}) collective-permute-start(f32[2,2048]{1,0:T(2,128)S(1)} %all_gather.12), channel_id=1, source_target_pairs={{0,4},{4,8},{8,12},{12,16},{16,20},{20,24},{24,28},{28,0},{1,5},{5... | collective-permute-start | bytes 49160 | tf_op jit(solution)/shard_map/ppermute | solution.py:16
  19.4 51.9 %copy-start.50 = (f32[1,1024]{1,0:T(1,128)}, f32[1,1024]{1,0:T(1,128)S(1)}, u32[]{:S(2)}) copy-start(f32[1,1024]{1,0:T(1,128)S(1)} %get-tuple-element.988) | copy-start | bytes 12292
  19.4 51.9 %copy-start.53 = (f32[1,1024]{1,0:T(1,128)}, f32[1,1024]{1,0:T(1,128)S(1)}, u32[]{:S(2)}) copy-start(f32[1,1024]{1,0:T(1,128)S(1)} %get-tuple-element.990) | copy-start | bytes 12292
  19.4 51.9 %copy-start.56 = (f32[1,1024]{1,0:T(1,128)}, f32[1,1024]{1,0:T(1,128)S(1)}, u32[]{:S(2)}) copy-start(f32[1,1024]{1,0:T(1,128)S(1)} %get-tuple-element.992) | copy-start | bytes 12292
  19.4 51.9 %copy-start.59 = (f32[1,1024]{1,0:T(1,128)}, f32[1,1024]{1,0:T(1,128)S(1)}, u32[]{:S(2)}) copy-start(f32[1,1024]{1,0:T(1,128)S(1)} %get-tuple-element.994) | copy-start | bytes 12292
  19.4 51.9 %copy-start.62 = (f32[1,1024]{1,0:T(1,128)}, f32[1,1024]{1,0:T(1,128)S(1)}, u32[]{:S(2)}) copy-start(f32[1,1024]{1,0:T(1,128)S(1)} %get-tuple-element.996) | copy-start | bytes 12292
  19.4 51.9 %copy-start.65 = (f32[1,1024]{1,0:T(1,128)}, f32[1,1024]{1,0:T(1,128)S(1)}, u32[]{:S(2)}) copy-start(f32[1,1024]{1,0:T(1,128)S(1)} %get-tuple-element.998) | copy-start | bytes 12292
  19.4 51.9 %copy-start.123 = (f32[1,1024]{1,0:T(1,128)}, f32[1,1024]{1,0:T(1,128)S(1)}, u32[]{:S(2)}) copy-start(f32[1,1024]{1,0:T(1,128)S(1)} %get-tuple-element.982) | copy-start | bytes 12292
  19.4 51.9 %copy-start.188 = (f32[1,1024]{1,0:T(1,128)}, f32[1,1024]{1,0:T(1,128)S(1)}, u32[]{:S(2)}) copy-start(f32[1,1024]{1,0:T(1,128)S(1)} %get-tuple-element.989) | copy-start | bytes 12292
  19.5 51.9 %copy-start.190 = (f32[1,1024]{1,0:T(1,128)}, f32[1,1024]{1,0:T(1,128)S(1)}, u32[]{:S(2)}) copy-start(f32[1,1024]{1,0:T(1,128)S(1)} %get-tuple-element.993) | copy-start | bytes 12292
  19.5 51.9 %copy-start.192 = (f32[1,1024]{1,0:T(1,128)}, f32[1,1024]{1,0:T(1,128)S(1)}, u32[]{:S(2)}) copy-start(f32[1,1024]{1,0:T(1,128)S(1)} %get-tuple-element.997) | copy-start | bytes 12292
  19.5 51.6 %copy-start = (f32[2,80,512]{2,1,0:T(8,128)S(1)}, f32[2,80,512]{2,1,0:T(8,128)}, u32[]{:S(2)}) copy-start(f32[2,80,512]{2,1,0:T(8,128)} %param.26) | copy-start | bytes 983044
  21.4 50.0 %copy-start.68 = (f32[1,1024]{1,0:T(1,128)}, f32[1,1024]{1,0:T(1,128)S(1)}, u32[]{:S(2)}) copy-start(f32[1,1024]{1,0:T(1,128)S(1)} %get-tuple-element.1001) | copy-start | bytes 12292
  21.4 50.0 %copy-start.71 = (f32[1,1024]{1,0:T(1,128)}, f32[1,1024]{1,0:T(1,128)S(1)}, u32[]{:S(2)}) copy-start(f32[1,1024]{1,0:T(1,128)S(1)} %get-tuple-element.1003) | copy-start | bytes 12292
  21.5 50.0 %copy-start.74 = (f32[1,1024]{1,0:T(1,128)}, f32[1,1024]{1,0:T(1,128)S(1)}, u32[]{:S(2)}) copy-start(f32[1,1024]{1,0:T(1,128)S(1)} %get-tuple-element.1005) | copy-start | bytes 12292
  21.5 50.0 %copy-start.77 = (f32[1,1024]{1,0:T(1,128)}, f32[1,1024]{1,0:T(1,128)S(1)}, u32[]{:S(2)}) copy-start(f32[1,1024]{1,0:T(1,128)S(1)} %get-tuple-element.1007) | copy-start | bytes 12292
  21.5 50.0 %copy-start.80 = (f32[1,1024]{1,0:T(1,128)}, f32[1,1024]{1,0:T(1,128)S(1)}, u32[]{:S(2)}) copy-start(f32[1,1024]{1,0:T(1,128)S(1)} %get-tuple-element.1009) | copy-start | bytes 12292
  21.5 50.0 %copy-start.83 = (f32[1,1024]{1,0:T(1,128)}, f32[1,1024]{1,0:T(1,128)S(1)}, u32[]{:S(2)}) copy-start(f32[1,1024]{1,0:T(1,128)S(1)} %get-tuple-element.1011) | copy-start | bytes 12292
  21.5 50.0 %copy-start.86 = (f32[1,1024]{1,0:T(1,128)}, f32[1,1024]{1,0:T(1,128)S(1)}, u32[]{:S(2)}) copy-start(f32[1,1024]{1,0:T(1,128)S(1)} %get-tuple-element.1013) | copy-start | bytes 12292
  21.5 50.0 %copy-start.89 = (f32[1,1024]{1,0:T(1,128)}, f32[1,1024]{1,0:T(1,128)S(1)}, u32[]{:S(2)}) copy-start(f32[1,1024]{1,0:T(1,128)S(1)} %get-tuple-element.1015) | copy-start | bytes 12292
  21.5 50.0 %copy-start.92 = (f32[1,1024]{1,0:T(1,128)}, f32[1,1024]{1,0:T(1,128)S(1)}, u32[]{:S(2)}) copy-start(f32[1,1024]{1,0:T(1,128)S(1)} %get-tuple-element.1017) | copy-start | bytes 12292
  23.3 48.2 %copy-start.95 = (f32[1,1024]{1,0:T(1,128)}, f32[1,1024]{1,0:T(1,128)S(1)}, u32[]{:S(2)}) copy-start(f32[1,1024]{1,0:T(1,128)S(1)} %get-tuple-element.1020) | copy-start | bytes 12292
  23.3 48.2 %copy-start.98 = (f32[1,1024]{1,0:T(1,128)}, f32[1,1024]{1,0:T(1,128)S(1)}, u32[]{:S(2)}) copy-start(f32[1,1024]{1,0:T(1,128)S(1)} %get-tuple-element.1022) | copy-start | bytes 12292
  23.3 48.2 %copy-start.101 = (f32[1,1024]{1,0:T(1,128)}, f32[1,1024]{1,0:T(1,128)S(1)}, u32[]{:S(2)}) copy-start(f32[1,1024]{1,0:T(1,128)S(1)} %get-tuple-element.1024) | copy-start | bytes 12292
  23.3 48.2 %copy-start.104 = (f32[1,1024]{1,0:T(1,128)}, f32[1,1024]{1,0:T(1,128)S(1)}, u32[]{:S(2)}) copy-start(f32[1,1024]{1,0:T(1,128)S(1)} %get-tuple-element.1026) | copy-start | bytes 12292
  34.8 36.8 %copy-start.129 = (f32[1,1024]{1,0:T(1,128)}, f32[1,1024]{1,0:T(1,128)S(1)}, u32[]{:S(2)}) copy-start(f32[1,1024]{1,0:T(1,128)S(1)} %get-tuple-element.967) | copy-start | bytes 12292
  34.8 36.8 %copy-start.131 = (f32[1,1024]{1,0:T(1,128)}, f32[1,1024]{1,0:T(1,128)S(1)}, u32[]{:S(2)}) copy-start(f32[1,1024]{1,0:T(1,128)S(1)} %get-tuple-element.968) | copy-start | bytes 12292
  34.8 36.8 %copy-start.133 = (f32[1,1024]{1,0:T(1,128)}, f32[1,1024]{1,0:T(1,128)S(1)}, u32[]{:S(2)}) copy-start(f32[1,1024]{1,0:T(1,128)S(1)} %get-tuple-element.969) | copy-start | bytes 12292
  34.9 36.8 %copy-start.135 = (f32[1,1024]{1,0:T(1,128)}, f32[1,1024]{1,0:T(1,128)S(1)}, u32[]{:S(2)}) copy-start(f32[1,1024]{1,0:T(1,128)S(1)} %get-tuple-element.970) | copy-start | bytes 12292
  34.9 36.8 %copy-start.137 = (f32[1,1024]{1,0:T(1,128)}, f32[1,1024]{1,0:T(1,128)S(1)}, u32[]{:S(2)}) copy-start(f32[1,1024]{1,0:T(1,128)S(1)} %get-tuple-element.971) | copy-start | bytes 12292
  34.9 36.8 %copy-start.139 = (f32[1,1024]{1,0:T(1,128)}, f32[1,1024]{1,0:T(1,128)S(1)}, u32[]{:S(2)}) copy-start(f32[1,1024]{1,0:T(1,128)S(1)} %get-tuple-element.972) | copy-start | bytes 12292
  34.9 36.8 %copy-start.141 = (f32[1,1024]{1,0:T(1,128)}, f32[1,1024]{1,0:T(1,128)S(1)}, u32[]{:S(2)}) copy-start(f32[1,1024]{1,0:T(1,128)S(1)} %get-tuple-element.973) | copy-start | bytes 12292
  34.9 36.8 %copy-start.143 = (f32[1,1024]{1,0:T(1,128)}, f32[1,1024]{1,0:T(1,128)S(1)}, u32[]{:S(2)}) copy-start(f32[1,1024]{1,0:T(1,128)S(1)} %get-tuple-element.974) | copy-start | bytes 12292
  34.9 36.8 %copy-start.145 = (f32[1,1024]{1,0:T(1,128)}, f32[1,1024]{1,0:T(1,128)S(1)}, u32[]{:S(2)}) copy-start(f32[1,1024]{1,0:T(1,128)S(1)} %get-tuple-element.975) | copy-start | bytes 12292
  34.9 36.8 %copy-start.147 = (f32[1,1024]{1,0:T(1,128)}, f32[1,1024]{1,0:T(1,128)S(1)}, u32[]{:S(2)}) copy-start(f32[1,1024]{1,0:T(1,128)S(1)} %get-tuple-element.976) | copy-start | bytes 12292
  34.9 36.8 %copy-start.149 = (f32[1,1024]{1,0:T(1,128)}, f32[1,1024]{1,0:T(1,128)S(1)}, u32[]{:S(2)}) copy-start(f32[1,1024]{1,0:T(1,128)S(1)} %get-tuple-element.977) | copy-start | bytes 12292
  34.9 36.8 %copy-start.151 = (f32[1,1024]{1,0:T(1,128)}, f32[1,1024]{1,0:T(1,128)S(1)}, u32[]{:S(2)}) copy-start(f32[1,1024]{1,0:T(1,128)S(1)} %get-tuple-element.978) | copy-start | bytes 12292
  34.9 36.8 %copy-start.153 = (f32[1,1024]{1,0:T(1,128)}, f32[1,1024]{1,0:T(1,128)S(1)}, u32[]{:S(2)}) copy-start(f32[1,1024]{1,0:T(1,128)S(1)} %get-tuple-element.979) | copy-start | bytes 12292
  108.2 9.5 %collective-permute-start.3 = (f32[8,4096]{1,0:T(8,128)S(1)}, f32[8,4096]{1,0:T(8,128)S(1)}, u32[]{:S(2)}, u32[]{:S(2)}) collective-permute-start(f32[8,4096]{1,0:T(8,128)S(1)} %all_gather.13), channel_id=1, source_target_pairs={{4,0},{8,4},{12,8},{16,12},{20,16},{24,20},{28,24},{0,28},{5,1},{9... | collective-permute-start | bytes 393224 | tf_op jit(solution)/shard_map/ppermute | solution.py:17
  108.2 9.5 %collective-permute-start.2 = (f32[8,4096]{1,0:T(8,128)S(1)}, f32[8,4096]{1,0:T(8,128)S(1)}, u32[]{:S(2)}, u32[]{:S(2)}) collective-permute-start(f32[8,4096]{1,0:T(8,128)S(1)} %all_gather.13), channel_id=1, source_target_pairs={{0,4},{4,8},{8,12},{12,16},{16,20},{20,24},{24,28},{28,0},{1,5},{5... | collective-permute-start | bytes 393224 | tf_op jit(solution)/shard_map/ppermute | solution.py:16
  149.0 1.4 collective-permute-start.5
  149.0 4.2 %collective-permute-start.4 = (f32[2,2048]{1,0:T(2,128)S(1)}, f32[2,2048]{1,0:T(2,128)S(1)}, u32[]{:S(2)}, u32[]{:S(2)}) collective-permute-start(f32[2,2048]{1,0:T(2,128)S(1)} %all_gather.14), channel_id=1, source_target_pairs={{0,4},{4,8},{8,12},{12,16},{16,20},{20,24},{24,28},{28,0},{1,5},{5... | collective-permute-start | bytes 49160 | tf_op jit(solution)/shard_map/ppermute | solution.py:16
  189.6 34.3 %collective-permute-start.7 = (f32[8,4096]{1,0:T(8,128)S(1)}, f32[8,4096]{1,0:T(8,128)S(1)}, u32[]{:S(2)}, u32[]{:S(2)}) collective-permute-start(f32[8,4096]{1,0:T(8,128)S(1)} %all_gather.15), channel_id=1, source_target_pairs={{4,0},{8,4},{12,8},{16,12},{20,16},{24,20},{28,24},{0,28},{5,1},{9... | collective-permute-start | bytes 393224 | tf_op jit(solution)/shard_map/ppermute | solution.py:17
  189.6 34.3 %collective-permute-start.6 = (f32[8,4096]{1,0:T(8,128)S(1)}, f32[8,4096]{1,0:T(8,128)S(1)}, u32[]{:S(2)}, u32[]{:S(2)}) collective-permute-start(f32[8,4096]{1,0:T(8,128)S(1)} %all_gather.15), channel_id=1, source_target_pairs={{0,4},{4,8},{8,12},{12,16},{16,20},{20,24},{24,28},{28,0},{1,5},{5... | collective-permute-start | bytes 393224 | tf_op jit(solution)/shard_map/ppermute | solution.py:16
  (181 other events, 2195.4 us)
where the time goes:
time: 247 us; the launch traced here: 243 us
  other arithmetic  91.4 us (37%)
  local copies, waits for them, and re-layouts  86.3 us (35%)
  blocking collectives  55.1 us (22%)
  between operations  5.39 us (2%)
  waiting for transfers between devices  3.08 us (1%)
    gather x4, local copies, waits for them, and re-layouts, remap(): return jnp.sum(weights[None] * values[:, places], axis=1)  47.4 us
    unnamed x114, other arithmetic  28.9 us
    all_gather x2, blocking collectives, per_device(): sea_block = lax.all_gather(sea_top, 'col', axis=1, tiled=True)  28.1 us
    all_gather x2, blocking collectives, per_device(): flux_block = lax.all_gather(fluxes, 'col', axis=1, tiled=True)  27 us
    add x22, other arithmetic, solve_columns(): pivot_value = 1.0 + lower_k + upper_k + lower_k * carry_c  26.1 us
    slice x4, local copies, waits for them, and re-layouts, solve_columns(): carry_d = (right_side[:, depth_index] + lower_k * carry_d) / pivot_value  12.2 us
    concatenate x4, local copies, waits for them, and re-layouts, extended(): value = jnp.concatenate([before, value, after], axis=dim)  11.7 us
    div x8, other arithmetic, solve_columns(): carry_d = (right_side[:, depth_index] + lower_k * carry_d) / pivot_value  10.5 us
  transfers between devices with their start and end apart: 8, of which 2 were waited for; matrix products, arithmetic and copies ran while one was open for 39% of the time, Pallas kernels for 0%

commit v1 on v0

--- a/solution.py
+++ b/solution.py
@@ -109,7 +109,14 @@
     air_span = air_cols * group_count
     for step_index in range(STEPS):
         sea_top = jnp.stack([sea_state[0, 0], ice_cover])
-        sea_block = lax.all_gather(sea_top, "col", axis=1, tiled=True)
+        devices = lax.axis_size("col")
+        route = [(i_2, (i_2 + 1) % devices) for i_2 in range(devices)]
+        pieces = [sea_top]
+        for stride in range(1, devices):
+            pieces = [lax.ppermute(pieces[0], "col", route), *pieces]
+        whole = jnp.concatenate(pieces, axis=1)
+        turn = (lax.axis_index("col") + 1) * pieces[-1].shape[1]
+        sea_block = jnp.roll(whole, turn, axis=1)
         sea_nearby = extended(sea_block, (("sec", 1),), sea_cols * group_count)
         air_sea = remap(sea_nearby, ocean_sources, ocean_weights)
         fluxes = surface_fluxes(air_state, air_sea, surface_forcing, air_mask)

time: 247 us -> 241 us (0.976)
  blocking collectives: 55.1 us -> 26.8 us
  waiting for transfers between devices: 3.08 us -> 26.1 us
  other arithmetic: 91.4 us -> 84.6 us
  starting transfers between devices: 2.04 us -> 7.06 us
    all_gather x2 -> x0, blocking collectives: 28.1 us -> none  [per_device(): sea_block = lax.all_gather(sea_top, 'col', axis=1, tiled=True)]
    ppermute x0 -> x6, waiting for transfers between devices: none -> 15.1 us  [per_device(): pieces = [lax.ppermute(pieces[0], 'col', route), *pieces]]
    ppermute x0 -> x6, starting transfers between devices: none -> 4.93 us  [per_device(): pieces = [lax.ppermute(pieces[0], 'col', route), *pieces]]
    ppermute x4, waiting for transfers between devices: 2.75 us -> 7.42 us  [extended(): before = lax.ppermute(last, axis, up)]
    unnamed x114, other arithmetic: 28.9 us -> 24.8 us
    ppermute x4, waiting for transfers between devices: 0.33 us -> 3.66 us  [extended(): after = lax.ppermute(leading, axis, down)]
    unnamed x555 -> x563, local copies, waits for them, and re-layouts: 4.5 us -> 5.12 us
  transfers between devices with their start and end apart: 8 -> 14, of which waited for: 2 -> 11; matrix products, arithmetic and copies ran while one was open for 39% -> 38% of each run, Pallas kernels for 0% -> 0%
where the time goes in v1:
time: 241 us; the launch traced here: 237 us
  local copies, waits for them, and re-layouts  86.7 us (36%)
  other arithmetic  84.6 us (35%)
  blocking collectives  26.8 us (11%)
  waiting for transfers between devices  26.1 us (11%)
  starting transfers between devices  7.06 us (3%)
  between operations  5.44 us (2%)
    gather x4, local copies, waits for them, and re-layouts, remap(): return jnp.sum(weights[None] * values[:, places], axis=1)  47.3 us
    all_gather x2, blocking collectives, per_device(): flux_block = lax.all_gather(fluxes, 'col', axis=1, tiled=True)  26.8 us
    add x22, other arithmetic, solve_columns(): pivot_value = 1.0 + lower_k + upper_k + lower_k * carry_c  26.5 us
    unnamed x114, other arithmetic  24.8 us
    ppermute x6, waiting for transfers between devices, per_device(): pieces = [lax.ppermute(pieces[0], 'col', route), *pieces]  15.1 us
    slice x4, local copies, waits for them, and re-layouts, solve_columns(): carry_d = (right_side[:, depth_index] + lower_k * carry_d) / pivot_value  12.2 us
    concatenate x4, local copies, waits for them, and re-layouts, extended(): value = jnp.concatenate([before, value, after], axis=dim)  11.6 us
    div x8, other arithmetic, solve_columns(): carry_d = (right_side[:, depth_index] + lower_k * carry_d) / pivot_value  10.2 us
  transfers between devices with their start and end apart: 14, of which 11 were waited for; matrix products, arithmetic and copies ran while one was open for 38% of the time, Pallas kernels for 0%

profile of v1, /device:TPU:0, one launch (start us, length us, event | category | flops | bytes accessed | tf_op | source)
XLA Modules:
  0.0 236.7 jit_solution(12256113815769741698)
XLA Ops:
  2.1 3.1 %collective-permute-start = (f32[2,512]{1,0:T(2,128)S(1)}, f32[2,512]{1,0:T(2,128)S(1)}, u32[]{:S(2)}, u32[]{:S(2)}) collective-permute-start(f32[2,512]{1,0:T(2,128)S(1)} %pad_maximum_fusion.4), channel_id=1, source_target_pairs={{0,1},{1,2},{2,3},{3,0},{4,5},{5,6},{6,7},{7,4},{8,9},{9,10},{10,1... | collective-permute-start | bytes 12296 | tf_op jit(solution)/shard_map/ppermute | solution.py:116
  5.1 1.9 fusion.475
  7.1 1.9 fusion.476
  9.1 1.8 fusion.477
  10.9 2.9 %negate_divide_fusion.20 = (f32[1,1024]{1,0:T(1,128)}, f32[1,1024]{1,0:T(1,128)}, f32[1,1024]{1,0:T(1,128)}, f32[1,1024]{1,0:T(1,128)}, f32[1,1024]{1,0:T(1,128)...) fusion(f32[64,1024]{1,0:T(8,128)} %param.23), kind=kLoop, calls=%fused_computation.1354 | loop fusion | flops 260096 | bytes 524288 | tf_op jit(solution)/shard_map/div | solution.py:33
  13.8 3.2 %fusion.470 = (f32[4,1,1024]{2,1,0:T(1,128)S(1)}, f32[4,1,1024]{2,1,0:T(1,128)}, f32[4,1,1024]{2,1,0:T(1,128)}, f32[4,1,1024]{2,1,0:T(1,128)}, f32[4,1,1024]{2,1...) fusion(f32[4,64,1024]{2,1,0:T(8,128)} %param.22), kind=kLoop, calls=%fused_computation.1800 | loop fusion | bytes 622592 | tf_op jit(solution)/shard_map/slice | solution.py:34
  17.1 3.4 %fusion.471 = (f32[4,1,1024]{2,1,0:T(1,128)}, f32[4,1,1024]{2,1,0:T(1,128)}, f32[4,1,1024]{2,1,0:T(1,128)S(1)}, f32[4,1,1024]{2,1,0:T(1,128)}, f32[4,1,1024]{2,1...) fusion(f32[4,64,1024]{2,1,0:T(8,128)} %param.22), kind=kLoop, calls=%fused_computation.1801 | loop fusion | bytes 622592 | tf_op jit(solution)/shard_map/slice | solution.py:34
  20.6 2.0 fusion.474
  22.6 1.4 fusion.473
  24.0 2.3 fusion.472
  26.3 3.3 %fusion.469 = (f32[4,1,1024]{2,1,0:T(1,128)}, f32[4,1,1024]{2,1,0:T(1,128)S(1)}, f32[4,1,1024]{2,1,0:T(1,128)}, f32[4,1,1024]{2,1,0:T(1,128)}, f32[4,1,1024]{2,1...) fusion(f32[4,64,1024]{2,1,0:T(8,128)} %param.22), kind=kLoop, calls=%fused_computation.1799 | loop fusion | bytes 622592 | tf_op jit(solution)/shard_map/slice | solution.py:34
  30.9 1.8 multiply_add_fusion.20
  35.2 1.3 multiply_add_fusion.17
  39.1 1.3 multiply_add_fusion.14
  40.4 1.3 multiply_add_fusion.13
  45.6 1.3 multiply_add_fusion.9
  49.5 1.3 multiply_add_fusion.6
  50.9 1.3 multiply_add_fusion.5
  56.0 1.6 collective-permute-start.1
  58.9 2.5 %collective-permute-done.1 = f32[2,512]{1,0:T(2,128)S(1)} collective-permute-done((f32[2,512]{1,0:T(2,128)S(1)}, f32[2,512]{1,0:T(2,128)S(1)}, u32[]{:S(2)}, u32[]{:S(2)}) %collective-permute-start.1) | collective-permute-done | bytes 4128 | tf_op jit(solution)/shard_map/ppermute | solution.py:116
  62.1 4.7 %collective-permute-done.2 = f32[2,512]{1,0:T(2,128)S(1)} collective-permute-done((f32[2,512]{1,0:T(2,128)S(1)}, f32[2,512]{1,0:T(2,128)S(1)}, u32[]{:S(2)}, u32[]{:S(2)}) %collective-permute-start.2) | collective-permute-done | bytes 4128 | tf_op jit(solution)/shard_map/ppermute | solution.py:116
  68.6 2.8 %collective-permute-done.3 = f32[2,2048]{1,0:T(2,128)S(1)} collective-permute-done((f32[2,2048]{1,0:T(2,128)S(1)}, f32[2,2048]{1,0:T(2,128)S(1)}, u32[]{:S(2)}, u32[]{:S(2)}) %collective-permute-start.3) | collective-permute-done | bytes 16416 | tf_op jit(solution)/shard_map/ppermute | solution.py:16
  72.0 1.8 copy.754
  73.8 15.4 %gather_fusion = f32[4096,2]{1,0:T(8,128)} fusion(f32[2,6144]{0,1:T(8,128)S(1)} %copy.754, s32[4096]{0:T(1024)} %bitcast_clamp_fusion), kind=kCustom, calls=%fused_computation | custom fusion | bytes 81920 | tf_op jit(solution)/shard_map/gather | solution.py:46
  89.3 2.0 multiply_reduce_fusion.1
  92.0 13.4 %all_gather.6 = f32[8,4096]{1,0:T(8,128)S(1)} all-gather(f32[8,1024]{1,0:T(8,128)S(1)} %stack.715), channel_id=1, replica_groups=mesh['sec'=8,'col'=4] {'col'}, dimensions={1}, use_global_device_ids=true | all-gather | bytes 163840 | tf_op jit(solution)/shard_map/all_gather | solution.py:123
  106.3 3.0 %collective-permute-done.6 = f32[8,4096]{1,0:T(8,128)S(1)} collective-permute-done((f32[8,4096]{1,0:T(8,128)S(1)}, f32[8,4096]{1,0:T(8,128)S(1)}, u32[]{:S(2)}, u32[]{:S(2)}) %collective-permute-start.6) | collective-permute-done | bytes 131104 | tf_op jit(solution)/shard_map/ppermute | solution.py:17
  109.3 1.9 collective-permute-done.5
  111.2 3.9 %copy.819 = f32[8,12288]{0,1:T(8,128)} copy(f32[8,12288]{1,0:T(8,128)S(1)} %pad_maximum_fusion) | data formatting | bytes 786432 | tf_op jit(solution)/shard_map/concatenate | solution.py:18
  115.2 8.3 %gather_fusion.1 = f32[2048,8]{1,0:T(8,128)S(1)} fusion(f32[8,12288]{0,1:T(8,128)} %copy.819, s32[2048]{0:T(1024)S(1)} %broadcast_clamp_fusion), kind=kCustom, calls=%fused_computation.1 | custom fusion | bytes 139264 | tf_op jit(solution)/shard_map/gather | solution.py:46
  130.3 1.7 fusion.109
  132.0 3.3 %collective-permute-done.7 = f32[2,512]{1,0:T(2,128)S(1)} collective-permute-done((f32[2,512]{1,0:T(2,128)S(1)}, f32[2,512]{1,0:T(2,128)S(1)}, u32[]{:S(2)}, u32[]{:S(2)}) %collective-permute-start.7) | collective-permute-done | bytes 4128 | tf_op jit(solution)/shard_map/ppermute | solution.py:116
  135.7 3.6 %multiply_subtract_fusion.103 = (f32[4,1024]{1,0:T(4,128)S(1)}, f32[4,1024]{1,0:T(4,128)}, f32[4,1024]{1,0:T(4,128)}, f32[4,1024]{1,0:T(4,128)}, f32[4,1024]{1,0...) fusion(f32[4,1024]{1,0:T(4,128)S(1)} %get-tuple-element.743, ...), kind=kLoop, calls=%fused_computation.750 | loop fusion | flops 1200128 | bytes 2097152 | tf_op jit(solution)/shard_map/sub | solution.py:40
  139.3 1.7 collective-permute-done.8
  141.6 2.0 add_divide_fusion.63
  143.6 2.8 %collective-permute-done.9 = f32[2,512]{1,0:T(2,128)S(1)} collective-permute-done((f32[2,512]{1,0:T(2,128)S(1)}, f32[2,512]{1,0:T(2,128)S(1)}, u32[]{:S(2)}, u32[]{:S(2)}) %collective-permute-start.9) | collective-permute-done | bytes 4128 | tf_op jit(solution)/shard_map/ppermute | solution.py:116
  148.1 2.7 %collective-permute-done.10 = f32[2,2048]{1,0:T(2,128)S(1)} collective-permute-done((f32[2,2048]{1,0:T(2,128)S(1)}, f32[2,2048]{1,0:T(2,128)S(1)}, u32[]{:S(2)}, u32[]{:S(2)}) %collective-permute-start.10) | collective-permute-done | bytes 16416 | tf_op jit(solution)/shard_map/ppermute | solution.py:16
  151.5 1.8 copy.901
  153.2 15.4 %gather_fusion.2 = f32[4096,2]{1,0:T(8,128)} fusion(f32[2,6144]{0,1:T(8,128)S(1)} %copy.901, s32[4096]{0:T(1024)} %bitcast_clamp_fusion), kind=kCustom, calls=%fused_computation.2 | custom fusion | bytes 81920 | tf_op jit(solution)/shard_map/gather | solution.py:46
  169.0 2.0 multiply_reduce_fusion
  173.8 13.4 %all_gather.7 = f32[8,4096]{1,0:T(8,128)S(1)} all-gather(f32[8,1024]{1,0:T(8,128)S(1)} %stack.831), channel_id=1, replica_groups=mesh['sec'=8,'col'=4] {'col'}, dimensions={1}, use_global_device_ids=true | all-gather | bytes 163840 | tf_op jit(solution)/shard_map/all_gather | solution.py:123
  188.0 3.1 %add_divide_fusion.38 = (f32[4,1,1024]{2,0,1:T(4,128)S(1)}, f32[4,1,1024]{2,0,1:T(4,128)S(1)}, f32[4,1,1024]{2,0,1:T(4,128)S(1)}, f32[4,1,1024]{2,0,1:T(4,128)S(...) fusion(f32[1024]{0:T(1024)} %bitcast.3426, ...), kind=kLoop, calls=%fused_computation.624 | loop fusion | flops 1093632 | bytes 2232320 | tf_op jit(solution)/shard_map/div | solution.py:34
  191.5 2.0 add_divide_fusion.60
  193.5 2.6 %constant_dynamic-update-slice_fusion.143 = (f32[4,64,1024]{2,0,1:T(4,128)S(1)}, f32[4,1024]{1,0:T(4,128)S(1)}, f32[4,1024]{1,0:T(4,128)S(1)}, f32[4,1024]{1,0:T...) fusion(f32[4,1024]{1,0:T(4,128)S(1)} %get-tuple-element.438, ...), kind=kLoop, calls=%fused_computation.155 | loop fusion | flops 1392639 | bytes 2138112
  196.5 3.4 %constant_dynamic-update-slice_fusion.142 = (f32[4,64,1024]{2,0,1:T(4,128)S(1)}, f32[4,1,1024]{2,0,1:T(4,128)S(1)}, f32[4,1,1024]{2,0,1:T(4,128)S(1)}, f32[4,1,1...) fusion(f32[4,64,1024]{2,0,1:T(4,128)S(1)} %get-tuple-element.40, ...), kind=kLoop, calls=%fused_computation.154 | loop fusion | flops 1454080 | bytes 2519040
  215.8 1.6 copy.904
  217.4 4.1 %copy.902 = f32[8,12288]{0,1:T(8,128)} copy(f32[8,12288]{1,0:T(8,128)S(1)} %pad_maximum_fusion.1) | data formatting | bytes 786432 | tf_op jit(solution)/shard_map/concatenate | solution.py:18
  221.6 8.3 %gather_fusion.3 = f32[2048,8]{1,0:T(8,128)S(1)} fusion(f32[8,12288]{0,1:T(8,128)} %copy.902, s32[2048]{0:T(1024)S(1)} %copy-done.200), kind=kCustom, calls=%fused_computation.3 | custom fusion | bytes 139264 | tf_op jit(solution)/shard_map/gather | solution.py:46
  (834 shorter events, 57.8 us)
Async XLA Ops:
  2.1 54.0 %collective-permute-start = (f32[2,512]{1,0:T(2,128)S(1)}, f32[2,512]{1,0:T(2,128)S(1)}, u32[]{:S(2)}, u32[]{:S(2)}) collective-permute-start(f32[2,512]{1,0:T(2,128)S(1)} %pad_maximum_fusion.4), channel_id=1, source_target_pairs={{0,1},{1,2},{2,3},{3,0},{4,5},{5,6},{6,7},{7,4},{8,9},{9,10},{10,1... | collective-permute-start | bytes 12296 | tf_op jit(solution)/shard_map/ppermute | solution.py:116
  7.0 54.5 %copy-start.117 = (f32[1,1024]{1,0:T(1,128)}, f32[1,1024]{1,0:T(1,128)S(1)}, u32[]{:S(2)}) copy-start(f32[1,1024]{1,0:T(1,128)S(1)} %get-tuple-element.983) | copy-start | bytes 12292
  7.0 134.0 %copy-start.49 = (f32[1,1024]{1,0:T(1,128)}, f32[1,1024]{1,0:T(1,128)S(1)}, u32[]{:S(2)}) copy-start(f32[1,1024]{1,0:T(1,128)S(1)} %get-tuple-element.989) | copy-start | bytes 12292
  7.0 134.0 %copy-start.51 = (f32[1,1024]{1,0:T(1,128)}, f32[1,1024]{1,0:T(1,128)S(1)}, u32[]{:S(2)}) copy-start(f32[1,1024]{1,0:T(1,128)S(1)} %get-tuple-element.991) | copy-start | bytes 12292
  7.0 134.0 %copy-start.53 = (f32[1,1024]{1,0:T(1,128)}, f32[1,1024]{1,0:T(1,128)S(1)}, u32[]{:S(2)}) copy-start(f32[1,1024]{1,0:T(1,128)S(1)} %get-tuple-element.993) | copy-start | bytes 12292
  7.0 134.0 %copy-start.55 = (f32[1,1024]{1,0:T(1,128)}, f32[1,1024]{1,0:T(1,128)S(1)}, u32[]{:S(2)}) copy-start(f32[1,1024]{1,0:T(1,128)S(1)} %get-tuple-element.995) | copy-start | bytes 12292
  7.0 134.0 %copy-start.57 = (f32[1,1024]{1,0:T(1,128)}, f32[1,1024]{1,0:T(1,128)S(1)}, u32[]{:S(2)}) copy-start(f32[1,1024]{1,0:T(1,128)S(1)} %get-tuple-element.997) | copy-start | bytes 12292
  7.0 134.0 %copy-start.59 = (f32[1,1024]{1,0:T(1,128)}, f32[1,1024]{1,0:T(1,128)S(1)}, u32[]{:S(2)}) copy-start(f32[1,1024]{1,0:T(1,128)S(1)} %get-tuple-element.999) | copy-start | bytes 12292
  7.1 59.8 %copy-start.211 = (f32[512]{0:T(512)S(1)}, f32[512]{0:T(512)}, u32[]{:S(2)}) copy-start(f32[512]{0:T(512)} %param.30) | copy-start | bytes 6148
  7.1 60.6 %copy-start.220 = (s32[4,512]{1,0:T(4,128)S(1)}, s32[4,512]{1,0:T(4,128)}, u32[]{:S(2)}) copy-start(s32[4,512]{1,0:T(4,128)} %param.32) | copy-start | bytes 24580
  9.0 120.8 %copy-start.65 = (f32[1,1024]{1,0:T(1,128)}, f32[1,1024]{1,0:T(1,128)S(1)}, u32[]{:S(2)}) copy-start(f32[1,1024]{1,0:T(1,128)S(1)} %get-tuple-element.1006) | copy-start | bytes 12292
  9.1 120.8 %copy-start.68 = (f32[1,1024]{1,0:T(1,128)}, f32[1,1024]{1,0:T(1,128)S(1)}, u32[]{:S(2)}) copy-start(f32[1,1024]{1,0:T(1,128)S(1)} %get-tuple-element.1008) | copy-start | bytes 12292
  9.1 120.8 %copy-start.71 = (f32[1,1024]{1,0:T(1,128)}, f32[1,1024]{1,0:T(1,128)S(1)}, u32[]{:S(2)}) copy-start(f32[1,1024]{1,0:T(1,128)S(1)} %get-tuple-element.1010) | copy-start | bytes 12292
  9.1 120.8 %copy-start.74 = (f32[1,1024]{1,0:T(1,128)}, f32[1,1024]{1,0:T(1,128)S(1)}, u32[]{:S(2)}) copy-start(f32[1,1024]{1,0:T(1,128)S(1)} %get-tuple-element.1012) | copy-start | bytes 12292
  9.1 132.0 %copy-start.61 = (f32[1,1024]{1,0:T(1,128)}, f32[1,1024]{1,0:T(1,128)S(1)}, u32[]{:S(2)}) copy-start(f32[1,1024]{1,0:T(1,128)S(1)} %get-tuple-element.1002) | copy-start | bytes 12292
  9.1 132.0 %copy-start.63 = (f32[1,1024]{1,0:T(1,128)}, f32[1,1024]{1,0:T(1,128)S(1)}, u32[]{:S(2)}) copy-start(f32[1,1024]{1,0:T(1,128)S(1)} %get-tuple-element.1004) | copy-start | bytes 12292
  10.9 50.6 %copy-start.92 = (f32[1,1024]{1,0:T(1,128)}, f32[1,1024]{1,0:T(1,128)S(1)}, u32[]{:S(2)}) copy-start(f32[1,1024]{1,0:T(1,128)S(1)} %get-tuple-element.1025) | copy-start | bytes 12292
  10.9 50.6 %copy-start.95 = (f32[1,1024]{1,0:T(1,128)}, f32[1,1024]{1,0:T(1,128)S(1)}, u32[]{:S(2)}) copy-start(f32[1,1024]{1,0:T(1,128)S(1)} %get-tuple-element.1027) | copy-start | bytes 12292
  17.0 124.1 %copy-start.5 = (f32[4,1,1024]{2,1,0:T(1,128)}, f32[4,1,1024]{2,1,0:T(1,128)S(1)}, u32[]{:S(2)}) copy-start(f32[4,1,1024]{2,1,0:T(1,128)S(1)} %get-tuple-element.920) | copy-start | bytes 49156
  17.0 124.1 %copy-start.7 = (f32[4,1,1024]{2,1,0:T(1,128)}, f32[4,1,1024]{2,1,0:T(1,128)S(1)}, u32[]{:S(2)}) copy-start(f32[4,1,1024]{2,1,0:T(1,128)S(1)} %get-tuple-element.922) | copy-start | bytes 49156
  17.0 124.1 %copy-start.9 = (f32[4,1,1024]{2,1,0:T(1,128)}, f32[4,1,1024]{2,1,0:T(1,128)S(1)}, u32[]{:S(2)}) copy-start(f32[4,1,1024]{2,1,0:T(1,128)S(1)} %get-tuple-element.924) | copy-start | bytes 49156
  17.0 124.1 %copy-start.11 = (f32[4,1,1024]{2,1,0:T(1,128)}, f32[4,1,1024]{2,1,0:T(1,128)S(1)}, u32[]{:S(2)}) copy-start(f32[4,1,1024]{2,1,0:T(1,128)S(1)} %get-tuple-element.926) | copy-start | bytes 49156
  17.0 124.1 %copy-start.13 = (f32[4,1,1024]{2,1,0:T(1,128)}, f32[4,1,1024]{2,1,0:T(1,128)S(1)}, u32[]{:S(2)}) copy-start(f32[4,1,1024]{2,1,0:T(1,128)S(1)} %get-tuple-element.928) | copy-start | bytes 49156
  17.1 124.1 %copy-start.15 = (f32[4,1,1024]{2,1,0:T(1,128)}, f32[4,1,1024]{2,1,0:T(1,128)S(1)}, u32[]{:S(2)}) copy-start(f32[4,1,1024]{2,1,0:T(1,128)S(1)} %get-tuple-element.930) | copy-start | bytes 49156
  17.1 124.1 %copy-start.17 = (f32[4,1,1024]{2,1,0:T(1,128)}, f32[4,1,1024]{2,1,0:T(1,128)S(1)}, u32[]{:S(2)}) copy-start(f32[4,1,1024]{2,1,0:T(1,128)S(1)} %get-tuple-element.932) | copy-start | bytes 49156
  20.5 120.6 %copy-start.19 = (f32[4,1,1024]{2,1,0:T(1,128)}, f32[4,1,1024]{2,1,0:T(1,128)S(1)}, u32[]{:S(2)}) copy-start(f32[4,1,1024]{2,1,0:T(1,128)S(1)} %get-tuple-element.935) | copy-start | bytes 49156
  20.5 120.6 %copy-start.21 = (f32[4,1,1024]{2,1,0:T(1,128)}, f32[4,1,1024]{2,1,0:T(1,128)S(1)}, u32[]{:S(2)}) copy-start(f32[4,1,1024]{2,1,0:T(1,128)S(1)} %get-tuple-element.937) | copy-start | bytes 49156
  20.5 120.6 %copy-start.23 = (f32[4,1,1024]{2,1,0:T(1,128)}, f32[4,1,1024]{2,1,0:T(1,128)S(1)}, u32[]{:S(2)}) copy-start(f32[4,1,1024]{2,1,0:T(1,128)S(1)} %get-tuple-element.939) | copy-start | bytes 49156
  20.5 120.6 %copy-start.25 = (f32[4,1,1024]{2,1,0:T(1,128)}, f32[4,1,1024]{2,1,0:T(1,128)S(1)}, u32[]{:S(2)}) copy-start(f32[4,1,1024]{2,1,0:T(1,128)S(1)} %get-tuple-element.941) | copy-start | bytes 49156
  20.5 120.6 %copy-start.27 = (f32[4,1,1024]{2,1,0:T(1,128)}, f32[4,1,1024]{2,1,0:T(1,128)S(1)}, u32[]{:S(2)}) copy-start(f32[4,1,1024]{2,1,0:T(1,128)S(1)} %get-tuple-element.943) | copy-start | bytes 49156
  20.6 120.6 %copy-start.29 = (f32[4,1,1024]{2,1,0:T(1,128)}, f32[4,1,1024]{2,1,0:T(1,128)S(1)}, u32[]{:S(2)}) copy-start(f32[4,1,1024]{2,1,0:T(1,128)S(1)} %get-tuple-element.945) | copy-start | bytes 49156
  20.6 120.6 %copy-start.31 = (f32[4,1,1024]{2,1,0:T(1,128)}, f32[4,1,1024]{2,1,0:T(1,128)S(1)}, u32[]{:S(2)}) copy-start(f32[4,1,1024]{2,1,0:T(1,128)S(1)} %get-tuple-element.947) | copy-start | bytes 49156
  20.6 120.6 %copy-start.33 = (f32[4,1,1024]{2,1,0:T(1,128)}, f32[4,1,1024]{2,1,0:T(1,128)S(1)}, u32[]{:S(2)}) copy-start(f32[4,1,1024]{2,1,0:T(1,128)S(1)} %get-tuple-element.949) | copy-start | bytes 49156
  20.6 120.6 %copy-start.35 = (f32[4,1,1024]{2,1,0:T(1,128)}, f32[4,1,1024]{2,1,0:T(1,128)S(1)}, u32[]{:S(2)}) copy-start(f32[4,1,1024]{2,1,0:T(1,128)S(1)} %get-tuple-element.951) | copy-start | bytes 49156
  26.3 114.9 %copy-start.3 = (f32[4,1,1024]{2,1,0:T(1,128)}, f32[4,1,1024]{2,1,0:T(1,128)S(1)}, u32[]{:S(2)}) copy-start(f32[4,1,1024]{2,1,0:T(1,128)S(1)} %get-tuple-element.956) | copy-start | bytes 49156
  56.0 5.4 %collective-permute-start.1 = (f32[2,512]{1,0:T(2,128)S(1)}, f32[2,512]{1,0:T(2,128)S(1)}, u32[]{:S(2)}, u32[]{:S(2)}) collective-permute-start(f32[2,512]{1,0:T(2,128)S(1)} %collective-permute-done), channel_id=1, source_target_pairs={{0,1},{1,2},{2,3},{3,0},{4,5},{5,6},{6,7},{7,4},{8,9},{9,10},{10,1... | collective-permute-start | bytes 12296 | tf_op jit(solution)/shard_map/ppermute | solution.py:116
  61.4 5.4 %collective-permute-start.2 = (f32[2,512]{1,0:T(2,128)S(1)}, f32[2,512]{1,0:T(2,128)S(1)}, u32[]{:S(2)}, u32[]{:S(2)}) collective-permute-start(f32[2,512]{1,0:T(2,128)S(1)} %collective-permute-done.1), channel_id=1, source_target_pairs={{0,1},{1,2},{2,3},{3,0},{4,5},{5,6},{6,7},{7,4},{8,9},{9,10},{10,1... | collective-permute-start | bytes 12296 | tf_op jit(solution)/shard_map/ppermute | solution.py:116
  67.1 1.5 collective-permute-start.4
  67.1 4.3 %collective-permute-start.3 = (f32[2,2048]{1,0:T(2,128)S(1)}, f32[2,2048]{1,0:T(2,128)S(1)}, u32[]{:S(2)}, u32[]{:S(2)}) collective-permute-start(f32[2,2048]{1,0:T(2,128)S(1)} %fusion.12), channel_id=1, source_target_pairs={{0,4},{4,8},{8,12},{12,16},{16,20},{20,24},{24,28},{28,0},{1,5},{5... | collective-permute-start | bytes 49160 | tf_op jit(solution)/shard_map/ppermute | solution.py:16
  105.4 3.8 %collective-permute-start.6 = (f32[8,4096]{1,0:T(8,128)S(1)}, f32[8,4096]{1,0:T(8,128)S(1)}, u32[]{:S(2)}, u32[]{:S(2)}) collective-permute-start(f32[8,4096]{1,0:T(8,128)S(1)} %all_gather.6), channel_id=1, source_target_pairs={{4,0},{8,4},{12,8},{16,12},{20,16},{24,20},{28,24},{0,28},{5,1},{9... | collective-permute-start | bytes 393224 | tf_op jit(solution)/shard_map/ppermute | solution.py:17
  105.4 5.8 %collective-permute-start.5 = (f32[8,4096]{1,0:T(8,128)S(1)}, f32[8,4096]{1,0:T(8,128)S(1)}, u32[]{:S(2)}, u32[]{:S(2)}) collective-permute-start(f32[8,4096]{1,0:T(8,128)S(1)} %all_gather.6), channel_id=1, source_target_pairs={{0,4},{4,8},{8,12},{12,16},{16,20},{20,24},{24,28},{28,0},{1,5},{5... | collective-permute-start | bytes 393224 | tf_op jit(solution)/shard_map/ppermute | solution.py:16
  129.6 5.6 %collective-permute-start.7 = (f32[2,512]{1,0:T(2,128)S(1)}, f32[2,512]{1,0:T(2,128)S(1)}, u32[]{:S(2)}, u32[]{:S(2)}) collective-permute-start(f32[2,512]{1,0:T(2,128)S(1)} %pad_maximum_fusion.5), channel_id=1, source_target_pairs={{0,1},{1,2},{2,3},{3,0},{4,5},{5,6},{6,7},{7,4},{8,9},{9,10},{10,1... | collective-permute-start | bytes 12296 | tf_op jit(solution)/shard_map/ppermute | solution.py:116
  135.5 5.5 %collective-permute-start.8 = (f32[2,512]{1,0:T(2,128)S(1)}, f32[2,512]{1,0:T(2,128)S(1)}, u32[]{:S(2)}, u32[]{:S(2)}) collective-permute-start(f32[2,512]{1,0:T(2,128)S(1)} %collective-permute-done.7), channel_id=1, source_target_pairs={{0,1},{1,2},{2,3},{3,0},{4,5},{5,6},{6,7},{7,4},{8,9},{9,10},{10,1... | collective-permute-start | bytes 12296 | tf_op jit(solution)/shard_map/ppermute | solution.py:116
  141.0 5.4 %collective-permute-start.9 = (f32[2,512]{1,0:T(2,128)S(1)}, f32[2,512]{1,0:T(2,128)S(1)}, u32[]{:S(2)}, u32[]{:S(2)}) collective-permute-start(f32[2,512]{1,0:T(2,128)S(1)} %collective-permute-done.8), channel_id=1, source_target_pairs={{0,1},{1,2},{2,3},{3,0},{4,5},{5,6},{6,7},{7,4},{8,9},{9,10},{10,1... | collective-permute-start | bytes 12296 | tf_op jit(solution)/shard_map/ppermute | solution.py:116
  146.6 1.5 collective-permute-start.11
  146.7 4.1 %collective-permute-start.10 = (f32[2,2048]{1,0:T(2,128)S(1)}, f32[2,2048]{1,0:T(2,128)S(1)}, u32[]{:S(2)}, u32[]{:S(2)}) collective-permute-start(f32[2,2048]{1,0:T(2,128)S(1)} %fusion.3), channel_id=1, source_target_pairs={{0,4},{4,8},{8,12},{12,16},{16,20},{20,24},{24,28},{28,0},{1,5},{5... | collective-permute-start | bytes 49160 | tf_op jit(solution)/shard_map/ppermute | solution.py:16
  187.1 30.2 %collective-permute-start.13 = (f32[8,4096]{1,0:T(8,128)S(1)}, f32[8,4096]{1,0:T(8,128)S(1)}, u32[]{:S(2)}, u32[]{:S(2)}) collective-permute-start(f32[8,4096]{1,0:T(8,128)S(1)} %all_gather.7), channel_id=1, source_target_pairs={{4,0},{8,4},{12,8},{16,12},{20,16},{24,20},{28,24},{0,28},{5,1},{9... | collective-permute-start | bytes 393224 | tf_op jit(solution)/shard_map/ppermute | solution.py:17
  187.1 30.2 %collective-permute-start.12 = (f32[8,4096]{1,0:T(8,128)S(1)}, f32[8,4096]{1,0:T(8,128)S(1)}, u32[]{:S(2)}, u32[]{:S(2)}) collective-permute-start(f32[8,4096]{1,0:T(8,128)S(1)} %all_gather.7), channel_id=1, source_target_pairs={{0,4},{4,8},{8,12},{12,16},{16,20},{20,24},{24,28},{28,0},{1,5},{5... | collective-permute-start | bytes 393224 | tf_op jit(solution)/shard_map/ppermute | solution.py:16
  (191 other events, 1983.5 us)
